TPU v7x, 256 devices: a whole 4x4x8 slice. The times are simulated.
256 devices in a mesh: grid: 16 (over y, x), mic: 4 (over z_hi), bin: 4 (over z_lo, core).
Axes of the slice: x: 4, y: 4, z: 8 (z_hi: 4, z_lo: 2; z = z_hi * 2 + z_lo), core: 2. Of those that a mesh axis runs over, the one named last changes fastest.
Arguments:
- grid_points: float32 [3, 16384], P(None, 'grid'), may hold values from -1 to 3, as said below
- mic_coords: float32 [3, 4096], P(None, 'mic'), may hold values from -1 to 1, as said below
- wavenumbers: float32 [16], P('bin'), may hold values from 20 to 150
- pressures: float32 [16, 2, 16, 4096], P('bin', None, None, 'mic'), may hold values from -6 to 6
Outputs:
- solution: float32 [16, 2, 16, 16384], P('bin', None, None, 'grid')
- residual: float32 [16, 2, 16, 4096], P('bin', None, None, 'mic')
Inputs may be any that keep to these rules, and one draw needn't show every extreme that they name: `grid_points`: rows 0 and 1 lie in -1 to 1, row 2 in 1 to 3. `mic_coords`: rows 0 and 1 lie in -1 to 1, row 2 in -0.05 to 0.05.
All inputs are finite; a program needn't handle non-finite values.
Results may differ from a plain program's by a relative error of at most 0.0055.
Values may be sent and summed in bfloat16 or wider, within the bound.
No kernel may reach another device: no remote copies, remote signals or barrier semaphores. Data moves between devices by JAX's collectives and lax.ppermute only.
A program may use at most 64 MiB of HBM per device.

v0:
```python
import math
import jax
import jax.numpy as jnp
from jax import lax
from jax.sharding import PartitionSpec as P

ITERS = 2


def steering_tiles(grid_points, mic_coords, wavenumbers, norm_scale):
    dist_x = grid_points[0][:, None] - mic_coords[0][None, :]
    dist_y = grid_points[1][:, None] - mic_coords[1][None, :]
    dist_z = grid_points[2][:, None] - mic_coords[2][None, :]
    radius = jnp.sqrt(dist_x * dist_x + dist_y * dist_y + dist_z * dist_z)
    amplitude = norm_scale / radius
    cos_list = []
    sin_list = []
    for bin_index in range(wavenumbers.shape[0]):
        phase_angle = wavenumbers[bin_index] * radius
        cos_list.append((jnp.cos(phase_angle) * amplitude).astype(jnp.bfloat16))
        sin_list.append((jnp.sin(phase_angle) * amplitude).astype(jnp.bfloat16))
    return (jnp.stack(cos_list), jnp.stack(sin_list))


def body(grid_points, mic_coords, wavenumbers, pressures):
    bin_count = pressures.shape[0]
    snap_count = pressures.shape[2]
    grid_local = grid_points.shape[1]
    norm_scale = 1.0 / math.sqrt(grid_local * lax.axis_size("grid"))
    cos_tiles, sin_tiles = steering_tiles(grid_points, mic_coords, wavenumbers, norm_scale)

    def combine_adjoint(cos_sum, sin_sum):
        real_part = cos_sum[:, :snap_count] - sin_sum[:, snap_count:]
        imag_part = cos_sum[:, snap_count:] + sin_sum[:, :snap_count]
        return jnp.stack([real_part, imag_part], axis=1)

    def apply_adjoint(residual):
        rounded = residual.astype(jnp.bfloat16).reshape(
            bin_count, 2 * snap_count, residual.shape[3]
        )
        cos_sum = jnp.einsum("fkm,fgm->fkg", rounded, cos_tiles, preferred_element_type=jnp.float32)
        sin_sum = jnp.einsum("fkm,fgm->fkg", rounded, sin_tiles, preferred_element_type=jnp.float32)
        partial_terms = combine_adjoint(cos_sum, sin_sum)
        summed = lax.psum(partial_terms, "mic")
        grad_norm = lax.psum(jnp.sum(summed * summed), ("grid", "bin"))
        return (summed, grad_norm)

    residual = pressures
    gradient, grad_norm = apply_adjoint(residual)
    direction = gradient
    solution = jnp.zeros_like(gradient)
    for iteration in range(ITERS):
        apply_rounded = direction.astype(jnp.bfloat16).reshape(
            bin_count, 2 * snap_count, direction.shape[3]
        )
        apply_cos_sum = jnp.einsum(
            "fkg,fgm->fkm", apply_rounded, cos_tiles, preferred_element_type=jnp.float32
        )
        apply_sin_sum = jnp.einsum(
            "fkg,fgm->fkm", apply_rounded, sin_tiles, preferred_element_type=jnp.float32
        )
        combine_real_part = apply_cos_sum[:, :snap_count] + apply_sin_sum[:, snap_count:]
        combine_imag_part = apply_cos_sum[:, snap_count:] - apply_sin_sum[:, :snap_count]
        apply_partial_terms = jnp.stack([combine_real_part, combine_imag_part], axis=1)
        apply_summed = lax.psum(apply_partial_terms, "grid")
        image_norm = lax.psum(jnp.sum(apply_summed * apply_summed), ("mic", "bin"))
        image, image_norm = (apply_summed, image_norm)
        step_size = grad_norm / image_norm
        solution = solution + step_size * direction
        residual = residual - step_size * image
        if iteration + 1 < ITERS:
            gradient, next_norm = apply_adjoint(residual)
            direction = gradient + next_norm / grad_norm * direction
            grad_norm = next_norm
    return (solution, residual)


def solution(mesh):
    placed = (P(None, "grid"), P(None, "mic"), P("bin"), P("bin", None, None, "mic"))
    return jax.shard_map(
        body,
        mesh=mesh,
        in_specs=placed,
        out_specs=(P("bin", None, None, "grid"), P("bin", None, None, "mic")),
        check_vma=False,
    )
```

profile of v0, /device:TPU:1, one launch (start us, length us, event | category | flops | bytes accessed | tf_op | source)
XLA Modules:
  0.0 768.9 jit_solution(6533060130410521625)
XLA Ops:
  7.2 0.0 all-reduce.5.cloned.1.call-start
  7.2 1.5 fusion.13
  8.7 0.8 fusion.11
  9.5 0.8 fusion.12
  10.4 1.1 convert_element_type.96
  11.5 67.4 %multiply_convert_fusion.7 = (bf16[1,1024,1024]{2,1,0:T(8,128)(2,1)S(1)}, bf16[1,1024,1024]{2,1,0:T(8,128)(2,1)S(1)}, bf16[1,1024,1024]{2,1,0:T(8,128)(2,1)S(1)}...) fusion(f32[1024]{0:T(1024)S(1)} %bitcast.62, ...), kind=kLoop, calls=%fused_computation.9 | loop fusion | flops 30408704 | bytes 16801808 | tf_op jit(solution)/shard_map/convert_element_type | solution.py:20
  78.9 2.4 pad_maximum_fusion
  81.3 0.0 copy-start
  81.3 0.0 copy-start.2
  81.3 2.6 convolution_bitcast_fusion
  83.9 0.6 copy-done
  84.5 2.5 copy-done.2
  87.0 2.6 convolution_bitcast_fusion.1
  89.6 0.1 fusion.8
  89.6 0.8 pad_maximum_fusion.2
  90.5 0.0 all-reduce.5.cloned.1.call-update
  90.5 0.0 all-reduce.7.cloned.1.call-start
  90.6 56.2 %all-reduce.5.cloned.1.call-done = f32[4,2,16,1024]{3,2,0,1:T(8,128)} async-done(((f32[4,2,16,1024]{3,2,0,1:T(8,128)}), f32[4,2,16,1024]{3,2,0,1:T(8,128)}) %all-reduce.5.cloned.1.call-update) | async-done | bytes 524304 | tf_op jit(solution)/shard_map/psum | solution.py:44
  146.7 1.9 multiply_reduce_fusion.3
  148.7 0.0 copy-start.1
  148.7 5.1 fusion.14
  153.8 0.7 copy-done.1
  154.5 0.0 copy-start.5
  154.5 1.5 fusion.15
  156.0 0.1 fusion.6
  156.1 0.8 pad_maximum_fusion.3
  156.9 0.0 all-reduce.7.cloned.1.call-update
  156.9 0.0 all-reduce.9.cloned.1.call-start
  157.0 94.4 %all-reduce.7.cloned.1.call-done = f32[4,2,16,1024]{3,2,0,1:T(8,128)} async-done(((f32[4,2,16,1024]{3,2,0,1:T(8,128)}), f32[4,2,16,1024]{3,2,0,1:T(8,128)}) %all-reduce.7.cloned.1.call-update) | async-done | bytes 524304 | tf_op jit(solution)/shard_map/psum | solution.py:65
  251.4 1.8 multiply_reduce_fusion.2
  253.2 140.4 %psum.57 = f32[]{:T(128)} all-reduce(f32[]{:T(128)} %get-tuple-element.14), channel_id=1, replica_groups=mesh['grid'=16,'mic'=4,'bin'=4] {'grid','bin'}, use_global_device_ids=true, to_apply=%region_2.0 | all-reduce | flops 1 | bytes 8 | tf_op jit(solution)/shard_map/psum | solution.py:45
  393.6 25.9 %psum.59 = f32[]{:T(128)} all-reduce(f32[]{:T(128)} %multiply_reduce_fusion.2), channel_id=1, replica_groups=mesh['grid'=16,'mic'=4,'bin'=4] {'mic','bin'}, use_global_device_ids=true, to_apply=%region_5.0 | all-reduce | flops 1 | bytes 8 | tf_op jit(solution)/shard_map/psum | solution.py:66
  420.8 0.0 copy-done.5
  420.8 1.1 fusion.10
  422.0 5.9 fusion.16
  427.9 0.0 copy-start.3
  427.9 6.0 fusion.17
  434.0 0.1 fusion.4
  434.0 0.8 pad_maximum_fusion.4
  434.9 0.0 all-reduce.9.cloned.1.call-update
  434.9 0.0 all-reduce.11.cloned.1.call-start
  434.9 47.9 %all-reduce.9.cloned.1.call-done = f32[4,2,16,1024]{3,2,0,1:T(8,128)} async-done(((f32[4,2,16,1024]{3,2,0,1:T(8,128)}), f32[4,2,16,1024]{3,2,0,1:T(8,128)}) %all-reduce.9.cloned.1.call-update) | async-done | bytes 524304 | tf_op jit(solution)/shard_map/psum | solution.py:44
  482.8 1.8 multiply_reduce_fusion.1
  484.6 140.7 %psum.61 = f32[]{:T(128)} all-reduce(f32[]{:T(128)} %multiply_reduce_fusion.1), channel_id=1, replica_groups=mesh['grid'=16,'mic'=4,'bin'=4] {'grid','bin'}, use_global_device_ids=true, to_apply=%region_8.0 | all-reduce | flops 1 | bytes 8 | tf_op jit(solution)/shard_map/psum | solution.py:45
  626.6 0.0 copy-done.3
  626.6 1.1 fusion.9
  627.8 4.9 fusion.18
  632.7 0.0 copy-start.6
  632.7 5.0 fusion.19
  637.7 0.0 copy-start.4
  637.7 0.1 fusion.2
  637.8 0.8 pad_maximum_fusion.5
  638.6 0.0 all-reduce.11.cloned.1.call-update
  638.6 91.7 %all-reduce.11.cloned.1.call-done = f32[4,2,16,1024]{3,2,0,1:T(8,128)} async-done(((f32[4,2,16,1024]{3,2,0,1:T(8,128)}), f32[4,2,16,1024]{3,2,0,1:T(8,128)}) %all-reduce.11.cloned.1.call-update) | async-done | bytes 524304 | tf_op jit(solution)/shard_map/psum | solution.py:65
  730.4 1.8 multiply_reduce_fusion
  732.1 26.0 %psum.63 = f32[]{:T(128)} all-reduce(f32[]{:T(128)} %multiply_reduce_fusion), channel_id=1, replica_groups=mesh['grid'=16,'mic'=4,'bin'=4] {'mic','bin'}, use_global_device_ids=true, to_apply=%region_11.0 | all-reduce | flops 1 | bytes 8 | tf_op jit(solution)/shard_map/psum | solution.py:66
  759.4 0.0 copy-done.6
  759.4 1.2 multiply_subtract_fusion
  760.6 0.8 copy.14
  761.5 0.0 copy-done.4
  761.5 0.1 multiply_add_fusion
  761.6 0.8 copy.13
  (3 shorter events, 0.1 us)
Async XLA Ops:
  7.2 139.6 %all-reduce.5.cloned.1.call-start = ((), (), s32[]{:S(2)}) async-start(), calls=%async_computation | async-start | bytes 1048576 | tf_op jit(solution)/shard_map/psum | solution.py:44
  81.3 3.2 copy-start
  81.3 5.7 copy-start.2
  90.5 160.9 %all-reduce.7.cloned.1.call-start = ((), (), s32[]{:S(2)}) async-start(), calls=%async_computation.1 | async-start | bytes 1048576 | tf_op jit(solution)/shard_map/psum | solution.py:65
  148.7 5.8 copy-start.1
  154.5 266.4 %copy-start.5 = (f32[4,2,16,1024]{3,2,1,0:T(8,128)S(1)}, f32[4,2,16,1024]{3,2,1,0:T(8,128)}, u32[]{:S(2)}) copy-start(f32[4,2,16,1024]{3,2,1,0:T(8,128)} %param.7) | copy-start | bytes 1572868
  156.9 325.9 %all-reduce.9.cloned.1.call-start = ((), (), s32[]{:S(2)}) async-start(), calls=%async_computation.2 | async-start | bytes 1048576 | tf_op jit(solution)/shard_map/psum | solution.py:44
  427.9 198.7 %copy-start.3 = (f32[4,2,16,1024]{3,2,0,1:T(8,128)S(1)}, f32[4,2,16,1024]{3,2,0,1:T(8,128)}, u32[]{:S(2)}) copy-start(f32[4,2,16,1024]{3,2,0,1:T(8,128)} %all-reduce.5.cloned.1.call-done) | copy-start | bytes 1572868
  434.9 295.5 %all-reduce.11.cloned.1.call-start = ((), (), s32[]{:S(2)}) async-start(), calls=%async_computation.3 | async-start | bytes 1048576 | tf_op jit(solution)/shard_map/psum | solution.py:65
  632.7 126.7 %copy-start.6 = (f32[4,2,16,1024]{3,2,0,1:T(8,128)S(1)}, f32[4,2,16,1024]{3,2,0,1:T(8,128)}, u32[]{:S(2)}) copy-start(f32[4,2,16,1024]{3,2,0,1:T(8,128)} %all-reduce.7.cloned.1.call-done) | copy-start | bytes 1572868
  637.7 123.8 %copy-start.4 = (f32[4,2,16,1024]{3,2,0,1:T(8,128)S(1)}, f32[4,2,16,1024]{3,2,0,1:T(8,128)}, u32[]{:S(2)}) copy-start(f32[4,2,16,1024]{3,2,0,1:T(8,128)} %all-reduce.9.cloned.1.call-done) | copy-start | bytes 1572868
Sparse Core Ops, SparseCore 0:
  90.6 56.0 all-reduce.4
  157.1 94.3 all-reduce.6
  435.0 47.7 all-reduce.8
  638.7 91.5 all-reduce.10
where the time goes:
time: 770 us; the launch traced here: 769 us
  blocking collectives  333 us (43%)
  waiting for transfers between devices  290 us (38%)
  other arithmetic  85.2 us (11%)
  matrix products  33.6 us (4%)
  between operations  17.9 us (2%)
  local copies, waits for them, and re-layouts  8.73 us (1%)
    psum x2, blocking collectives, apply_adjoint(): grad_norm = lax.psum(jnp.sum(summed * summed), ('grid', 'bin'))  281 us
    psum x2, waiting for transfers between devices, body(): apply_summed = lax.psum(apply_partial_terms, 'grid')  186 us
    psum x2, waiting for transfers between devices, apply_adjoint(): summed = lax.psum(partial_terms, 'mic')  104 us
    convert_element_type x1, other arithmetic, steering_tiles(): cos_list.append((jnp.cos(phase_angle) * amplitude).astype(jnp.bfloat16))  67.4 us
    psum x2, blocking collectives, body(): image_norm = lax.psum(jnp.sum(apply_summed * apply_summed), ('mic', 'bin'))  51.9 us
  transfers between devices with their start and end apart: 4, of which 4 were waited for; matrix products, arithmetic and copies ran while one was open for 0% of the time, Pallas kernels for 0%

commit v1 on v0

--- a/solution.py
+++ b/solution.py
@@ -62,7 +62,11 @@
         combine_real_part = apply_cos_sum[:, :snap_count] + apply_sin_sum[:, snap_count:]
         combine_imag_part = apply_cos_sum[:, snap_count:] - apply_sin_sum[:, :snap_count]
         apply_partial_terms = jnp.stack([combine_real_part, combine_imag_part], axis=1)
-        apply_summed = lax.psum(apply_partial_terms, "grid")
+        apply_summed = apply_partial_terms
+        for hop in (1, 2, 4, 8):
+            apply_summed = apply_summed + lax.ppermute(
+                apply_summed, "grid", [(dev, dev ^ hop) for dev in range(16)]
+            )
         image_norm = lax.psum(jnp.sum(apply_summed * apply_summed), ("mic", "bin"))
         image, image_norm = (apply_summed, image_norm)
         step_size = grad_norm / image_norm

time: 770 us -> 664 us (0.86)
  waiting for transfers between devices: 290 us -> 165 us
  starting transfers between devices: 0.16 us -> 15.4 us
  blocking collectives: 333 us -> 341 us
    psum x2 -> x0, waiting for transfers between devices: 186 us -> none  [body(): apply_summed = lax.psum(apply_partial_terms, 'grid')]
    ppermute x0 -> x8, waiting for transfers between devices: none -> 62.8 us  [body(): lax.ppermute(apply_summed, 'grid', [(dev, dev ^ hop) for dev in range(16)])]
    ppermute x0 -> x8, starting transfers between devices: none -> 15.3 us  [body(): lax.ppermute(apply_summed, 'grid', [(dev, dev ^ hop) for dev in range(16)])]
  transfers between devices with their start and end apart: 4 -> 10, of which waited for: 4 -> 9; matrix products, arithmetic and copies ran while one was open for 0% -> 0% of each run, Pallas kernels for 0% -> 0%
where the time goes in v1:
time: 664 us; the launch traced here: 662 us
  blocking collectives  341 us (51%)
  waiting for transfers between devices  165 us (25%)
  other arithmetic  80.1 us (12%)
  matrix products  33.5 us (5%)
  between operations  18.3 us (3%)
  starting transfers between devices  15.4 us (2%)
  local copies, waits for them, and re-layouts  8.73 us (1%)
    psum x2, blocking collectives, apply_adjoint(): grad_norm = lax.psum(jnp.sum(summed * summed), ('grid', 'bin'))  284 us
    psum x2, waiting for transfers between devices, apply_adjoint(): summed = lax.psum(partial_terms, 'mic')  102 us
    convert_element_type x1, other arithmetic, steering_tiles(): cos_list.append((jnp.cos(phase_angle) * amplitude).astype(jnp.bfloat16))  67.5 us
    ppermute x8, waiting for transfers between devices, body(): lax.ppermute(apply_summed, 'grid', [(dev, dev ^ hop) for dev in range(16)])  62.8 us
    psum x2, blocking collectives, body(): image_norm = lax.psum(jnp.sum(apply_summed * apply_summed), ('mic', 'bin'))  56.9 us
    ppermute x8, starting transfers between devices, body(): lax.ppermute(apply_summed, 'grid', [(dev, dev ^ hop) for dev in range(16)])  15.3 us
  transfers between devices with their start and end apart: 10, of which 9 were waited for; matrix products, arithmetic and copies ran while one was open for 0% of the time, Pallas kernels for 0%

profile of v1, /device:TPU:1, one launch (start us, length us, event | category | flops | bytes accessed | tf_op | source)
XLA Modules:
  0.0 662.4 jit_solution(17077937740760529066)
XLA Ops:
  7.2 0.0 all-reduce.3.cloned.1.call-start
  7.2 1.5 fusion.15
  8.7 0.8 fusion.13
  9.5 0.8 fusion.14
  10.4 1.1 convert_element_type.96
  11.4 67.5 %multiply_convert_fusion.7 = (bf16[1,1024,1024]{2,1,0:T(8,128)(2,1)S(1)}, bf16[1,1024,1024]{2,1,0:T(8,128)(2,1)S(1)}, bf16[1,1024,1024]{2,1,0:T(8,128)(2,1)S(1)}...) fusion(f32[1024]{0:T(1024)S(1)} %bitcast.62, ...), kind=kLoop, calls=%fused_computation.9 | loop fusion | flops 30408704 | bytes 16801808 | tf_op jit(solution)/shard_map/convert_element_type | solution.py:20
  78.9 2.4 pad_maximum_fusion
  81.3 2.6 convolution_bitcast_fusion
  83.9 0.6 copy-done
  84.5 2.5 copy-done.2
  87.0 2.6 convolution_bitcast_fusion.1
  89.6 0.1 fusion.8
  89.7 0.8 pad_maximum_fusion.2
  90.5 0.0 all-reduce.3.cloned.1.call-update
  90.5 0.0 all-reduce.5.cloned.1.call-start
  90.6 56.0 %all-reduce.3.cloned.1.call-done = f32[4,2,16,1024]{3,2,0,1:T(8,128)} async-done(((f32[4,2,16,1024]{3,2,0,1:T(8,128)}), f32[4,2,16,1024]{3,2,0,1:T(8,128)}) %all-reduce.3.cloned.1.call-update) | async-done | bytes 524304 | tf_op jit(solution)/shard_map/psum | solution.py:44
  146.6 1.9 multiply_reduce_fusion.3
  148.6 5.1 fusion.16
  153.7 0.7 copy-done.1
  154.3 1.5 fusion.17
  155.9 0.1 fusion.6
  156.0 1.4 collective-permute-start
  157.4 9.9 %collective-permute-done = f32[4,2,16,1024]{3,2,0,1:T(8,128)S(1)} collective-permute-done((f32[4,2,16,1024]{3,2,0,1:T(8,128)S(1)}, f32[4,2,16,1024]{3,2,0,1:T(8,128)S(1)}, u32[]{:S(2)}, u32[]{:S(2)}) %collective-permute-start) | collective-permute-done | bytes 524320 | tf_op jit(solution)/shard_map/ppermute | solution.py:67
  167.3 0.1 fusion.12
  167.4 2.9 collective-permute-start.1
  170.3 10.1 %collective-permute-done.1 = f32[4,2,16,1024]{3,2,0,1:T(8,128)S(1)} collective-permute-done((f32[4,2,16,1024]{3,2,0,1:T(8,128)S(1)}, f32[4,2,16,1024]{3,2,0,1:T(8,128)S(1)}, u32[]{:S(2)}, u32[]{:S(2)}) %collective-permute-start.1) | collective-permute-done | bytes 524320 | tf_op jit(solution)/shard_map/ppermute | solution.py:67
  180.5 0.1 fusion.39
  180.6 1.2 collective-permute-start.2
  181.7 8.9 %collective-permute-done.2 = f32[4,2,16,1024]{3,2,0,1:T(8,128)S(1)} collective-permute-done((f32[4,2,16,1024]{3,2,0,1:T(8,128)S(1)}, f32[4,2,16,1024]{3,2,0,1:T(8,128)S(1)}, u32[]{:S(2)}, u32[]{:S(2)}) %collective-permute-start.2) | collective-permute-done | bytes 524320 | tf_op jit(solution)/shard_map/ppermute | solution.py:67
  190.6 0.1 add.136
  190.7 2.6 collective-permute-start.3
  193.3 143.7 %psum.43 = f32[]{:T(128)} all-reduce(f32[]{:T(128)} %get-tuple-element.18), channel_id=1, replica_groups=mesh['grid'=16,'mic'=4,'bin'=4] {'grid','bin'}, use_global_device_ids=true, to_apply=%region_2.0 | all-reduce | flops 1 | bytes 8 | tf_op jit(solution)/shard_map/psum | solution.py:45
  337.0 0.8 multiply_reduce_fusion.2
  337.8 24.2 %psum.44 = f32[]{:T(128)} all-reduce(f32[]{:T(128)} %get-tuple-element.8), channel_id=1, replica_groups=mesh['grid'=16,'mic'=4,'bin'=4] {'mic','bin'}, use_global_device_ids=true, to_apply=%region_4.0 | all-reduce | flops 1 | bytes 8 | tf_op jit(solution)/shard_map/psum | solution.py:70
  363.4 0.1 fusion.10
  363.5 5.9 fusion.18
  369.5 6.0 fusion.19
  375.5 0.1 fusion.4
  375.6 0.8 pad_maximum_fusion.4
  376.4 0.0 all-reduce.5.cloned.1.call-update
  376.4 46.2 %all-reduce.5.cloned.1.call-done = f32[4,2,16,1024]{3,2,0,1:T(8,128)} async-done(((f32[4,2,16,1024]{3,2,0,1:T(8,128)}), f32[4,2,16,1024]{3,2,0,1:T(8,128)}) %all-reduce.5.cloned.1.call-update) | async-done | bytes 524304 | tf_op jit(solution)/shard_map/psum | solution.py:44
  422.7 1.8 multiply_reduce_fusion.1
  424.4 140.6 %psum.46 = f32[]{:T(128)} all-reduce(f32[]{:T(128)} %multiply_reduce_fusion.1), channel_id=1, replica_groups=mesh['grid'=16,'mic'=4,'bin'=4] {'grid','bin'}, use_global_device_ids=true, to_apply=%region_7.0 | all-reduce | flops 1 | bytes 8 | tf_op jit(solution)/shard_map/psum | solution.py:45
  566.4 1.1 fusion.9
  567.5 4.9 fusion.20
  572.5 4.9 fusion.21
  577.4 0.1 fusion.2
  577.5 0.1 collective-permute-start.4
  577.6 8.6 %collective-permute-done.4 = f32[4,2,16,1024]{3,2,0,1:T(8,128)S(1)} collective-permute-done((f32[4,2,16,1024]{3,2,0,1:T(8,128)S(1)}, f32[4,2,16,1024]{3,2,0,1:T(8,128)S(1)}, u32[]{:S(2)}, u32[]{:S(2)}) %collective-permute-start.4) | collective-permute-done | bytes 524320 | tf_op jit(solution)/shard_map/ppermute | solution.py:67
  586.2 0.1 fusion.11
  586.3 0.1 collective-permute-start.5
  586.4 9.5 %collective-permute-done.5 = f32[4,2,16,1024]{3,2,0,1:T(8,128)S(1)} collective-permute-done((f32[4,2,16,1024]{3,2,0,1:T(8,128)S(1)}, f32[4,2,16,1024]{3,2,0,1:T(8,128)S(1)}, u32[]{:S(2)}, u32[]{:S(2)}) %collective-permute-start.5) | collective-permute-done | bytes 524320 | tf_op jit(solution)/shard_map/ppermute | solution.py:67
  595.9 0.1 fusion.38
  596.0 0.1 collective-permute-start.6
  596.1 8.3 %collective-permute-done.6 = f32[4,2,16,1024]{3,2,0,1:T(8,128)S(1)} collective-permute-done((f32[4,2,16,1024]{3,2,0,1:T(8,128)S(1)}, f32[4,2,16,1024]{3,2,0,1:T(8,128)S(1)}, u32[]{:S(2)}, u32[]{:S(2)}) %collective-permute-start.6) | collective-permute-done | bytes 524320 | tf_op jit(solution)/shard_map/ppermute | solution.py:67
  604.4 0.1 add.143
  604.5 6.9 %collective-permute-start.7 = (f32[4,2,16,1024]{3,2,0,1:T(8,128)S(1)}, f32[4,2,16,1024]{3,2,0,1:T(8,128)S(1)}, u32[]{:S(2)}, u32[]{:S(2)}) collective-permute-start(f32[4,2,16,1024]{3,2,0,1:T(8,128)S(1)} %add.143), channel_id=1, source_target_pairs={{0,128},{16,144},{32,160},{48,176},{64,192},{80,208},{96,224},{112... | collective-permute-start | bytes 1572872 | tf_op jit(solution)/shard_map/ppermute | solution.py:67
  611.4 7.4 %collective-permute-done.7 = f32[4,2,16,1024]{3,2,0,1:T(8,128)S(1)} collective-permute-done((f32[4,2,16,1024]{3,2,0,1:T(8,128)S(1)}, f32[4,2,16,1024]{3,2,0,1:T(8,128)S(1)}, u32[]{:S(2)}, u32[]{:S(2)}) %collective-permute-start.7) | collective-permute-done | bytes 524320 | tf_op jit(solution)/shard_map/ppermute | solution.py:67
  618.8 0.8 multiply_reduce_fusion
  619.6 32.7 %psum.47 = f32[]{:T(128)} all-reduce(f32[]{:T(128)} %get-tuple-element.6), channel_id=1, replica_groups=mesh['grid'=16,'mic'=4,'bin'=4] {'mic','bin'}, use_global_device_ids=true, to_apply=%region_9.0 | all-reduce | flops 1 | bytes 8 | tf_op jit(solution)/shard_map/psum | solution.py:70
  653.6 0.1 multiply_subtract_fusion
  653.7 0.8 copy.14
  654.6 0.1 multiply_add_fusion
  654.7 0.8 copy.13
  (15 shorter events, 0.2 us)
Async XLA Ops:
  7.2 139.4 %all-reduce.3.cloned.1.call-start = ((), (), s32[]{:S(2)}) async-start(), calls=%async_computation | async-start | bytes 1048576 | tf_op jit(solution)/shard_map/psum | solution.py:44
  81.3 3.2 copy-start
  81.3 5.7 copy-start.2
  90.5 332.1 %all-reduce.5.cloned.1.call-start = ((), (), s32[]{:S(2)}) async-start(), calls=%async_computation.1 | async-start | bytes 1048576 | tf_op jit(solution)/shard_map/psum | solution.py:44
  148.6 5.8 copy-start.1
  156.0 207.4 %copy-start.5 = (f32[4,2,16,1024]{3,2,1,0:T(8,128)S(1)}, f32[4,2,16,1024]{3,2,1,0:T(8,128)}, u32[]{:S(2)}) copy-start(f32[4,2,16,1024]{3,2,1,0:T(8,128)} %param.7) | copy-start | bytes 1572868
  156.0 11.3 %collective-permute-start = (f32[4,2,16,1024]{3,2,0,1:T(8,128)S(1)}, f32[4,2,16,1024]{3,2,0,1:T(8,128)S(1)}, u32[]{:S(2)}, u32[]{:S(2)}) collective-permute-start(f32[4,2,16,1024]{3,2,0,1:T(8,128)S(1)} %pad_maximum_fusion.3), channel_id=1, source_target_pairs={{0,16},{16,0},{32,48},{48,32},{64,80},{80,64},{96,112},{112,96},{1... | collective-permute-start | bytes 1572872 | tf_op jit(solution)/shard_map/ppermute | solution.py:67
  167.4 13.1 %collective-permute-start.1 = (f32[4,2,16,1024]{3,2,0,1:T(8,128)S(1)}, f32[4,2,16,1024]{3,2,0,1:T(8,128)S(1)}, u32[]{:S(2)}, u32[]{:S(2)}) collective-permute-start(f32[4,2,16,1024]{3,2,0,1:T(8,128)S(1)} %fusion.12), channel_id=1, source_target_pairs={{0,32},{16,48},{32,0},{48,16},{64,96},{80,112},{96,64},{112,80},{1... | collective-permute-start | bytes 1572872 | tf_op jit(solution)/shard_map/ppermute | solution.py:67
  180.6 10.1 %collective-permute-start.2 = (f32[4,2,16,1024]{3,2,0,1:T(8,128)S(1)}, f32[4,2,16,1024]{3,2,0,1:T(8,128)S(1)}, u32[]{:S(2)}, u32[]{:S(2)}) collective-permute-start(f32[4,2,16,1024]{3,2,0,1:T(8,128)S(1)} %fusion.39), channel_id=1, source_target_pairs={{0,64},{16,80},{32,96},{48,112},{64,0},{80,16},{96,32},{112,48},{1... | collective-permute-start | bytes 1572872 | tf_op jit(solution)/shard_map/ppermute | solution.py:67
  190.7 146.3 %collective-permute-start.3 = (f32[4,2,16,1024]{3,2,0,1:T(8,128)S(1)}, f32[4,2,16,1024]{3,2,0,1:T(8,128)S(1)}, u32[]{:S(2)}, u32[]{:S(2)}) collective-permute-start(f32[4,2,16,1024]{3,2,0,1:T(8,128)S(1)} %add.136), channel_id=1, source_target_pairs={{0,128},{16,144},{32,160},{48,176},{64,192},{80,208},{96,224},{112... | collective-permute-start | bytes 1572872 | tf_op jit(solution)/shard_map/ppermute | solution.py:67
  369.5 196.9 %copy-start.3 = (f32[4,2,16,1024]{3,2,0,1:T(8,128)S(1)}, f32[4,2,16,1024]{3,2,0,1:T(8,128)}, u32[]{:S(2)}) copy-start(f32[4,2,16,1024]{3,2,0,1:T(8,128)} %all-reduce.3.cloned.1.call-done) | copy-start | bytes 1572868
  577.5 8.7 %collective-permute-start.4 = (f32[4,2,16,1024]{3,2,0,1:T(8,128)S(1)}, f32[4,2,16,1024]{3,2,0,1:T(8,128)S(1)}, u32[]{:S(2)}, u32[]{:S(2)}) collective-permute-start(f32[4,2,16,1024]{3,2,0,1:T(8,128)S(1)} %pad_maximum_fusion.5), channel_id=1, source_target_pairs={{0,16},{16,0},{32,48},{48,32},{64,80},{80,64},{96,112},{112,96},{1... | collective-permute-start | bytes 1572872 | tf_op jit(solution)/shard_map/ppermute | solution.py:67
  586.3 68.3 %copy-start.4 = (f32[4,2,16,1024]{3,2,0,1:T(8,128)S(1)}, f32[4,2,16,1024]{3,2,0,1:T(8,128)}, u32[]{:S(2)}) copy-start(f32[4,2,16,1024]{3,2,0,1:T(8,128)} %all-reduce.5.cloned.1.call-done) | copy-start | bytes 1572868
  586.3 9.6 %collective-permute-start.5 = (f32[4,2,16,1024]{3,2,0,1:T(8,128)S(1)}, f32[4,2,16,1024]{3,2,0,1:T(8,128)S(1)}, u32[]{:S(2)}, u32[]{:S(2)}) collective-permute-start(f32[4,2,16,1024]{3,2,0,1:T(8,128)S(1)} %fusion.11), channel_id=1, source_target_pairs={{0,32},{16,48},{32,0},{48,16},{64,96},{80,112},{96,64},{112,80},{1... | collective-permute-start | bytes 1572872 | tf_op jit(solution)/shard_map/ppermute | solution.py:67
  596.0 8.4 %collective-permute-start.6 = (f32[4,2,16,1024]{3,2,0,1:T(8,128)S(1)}, f32[4,2,16,1024]{3,2,0,1:T(8,128)S(1)}, u32[]{:S(2)}, u32[]{:S(2)}) collective-permute-start(f32[4,2,16,1024]{3,2,0,1:T(8,128)S(1)} %fusion.38), channel_id=1, source_target_pairs={{0,64},{16,80},{32,96},{48,112},{64,0},{80,16},{96,32},{112,48},{1... | collective-permute-start | bytes 1572872 | tf_op jit(solution)/shard_map/ppermute | solution.py:67
  604.5 14.3 %collective-permute-start.7 = (f32[4,2,16,1024]{3,2,0,1:T(8,128)S(1)}, f32[4,2,16,1024]{3,2,0,1:T(8,128)S(1)}, u32[]{:S(2)}, u32[]{:S(2)}) collective-permute-start(f32[4,2,16,1024]{3,2,0,1:T(8,128)S(1)} %add.143), channel_id=1, source_target_pairs={{0,128},{16,144},{32,160},{48,176},{64,192},{80,208},{96,224},{112... | collective-permute-start | bytes 1572872 | tf_op jit(solution)/shard_map/ppermute | solution.py:67
Sparse Core Ops, SparseCore 0:
  90.6 55.9 all-reduce.2
  376.5 46.0 all-reduce.4
